TPU v7x, 32 devices: a whole 2x2x4 slice. The times are simulated.
32 devices in a mesh: prow: 8 (over z, x), pcol: 4 (over y, core).
Axes of the slice: x: 2, y: 2, z: 4, core: 2. Of those that a mesh axis runs over, the one named last changes fastest.
Arguments:
- panel: float32 [8192, 128], P('prow'), may hold values from -1.8765018 to 11.876502
- trailing: float32 [8192, 8192], P('prow', 'pcol'), may hold values from -8 to 8
Outputs:
- updated: float32 [8192, 8192], P('prow', 'pcol')
- band_block: float32 [128, 128], replicated
All inputs are finite; a program needn't handle non-finite values.
Results may differ from a plain program's by a relative error of at most 0.00012.
Values sent between devices are 32-bit elements; how exact they have to be, the bound alone decides.
A program may use at most 128 MiB of HBM per device.

v0:
```python
import functools

import jax
import jax.numpy as jnp
from jax import lax
from jax.experimental import pallas as pl
from jax.experimental.pallas import tpu as pltpu
from jax.sharding import PartitionSpec as P

STEPS = 16


def factor_body(gram, top_t, between):
    size = gram.shape[0]
    rows = lax.broadcasted_iota(jnp.int32, (size, size), 0)
    cols = lax.broadcasted_iota(jnp.int32, (size, size), 1)

    def block(turn, carry):
        work, other = carry
        between(turn)
        live = size - turn * STEPS
        for k in range(STEPS):
            at_col = cols == k
            below = jnp.logical_and(rows > k, rows < live)
            col = jnp.broadcast_to(work[:, k : k + 1], (size, size))
            row_scale = lax.rsqrt(col[k : k + 1, :])
            row = jnp.where(at_col[:1], 1.0, work[k : k + 1, :]) * row_scale
            low = jnp.where(jnp.logical_and(rows >= k, rows < live), col * row_scale, 0.0)
            work = jnp.where(
                rows == k,
                row,
                jnp.where(below, jnp.where(at_col, 0.0, work) - low * row, work),
            )
            ocol = jnp.broadcast_to(other[:, k : k + 1], (size, size)) + low
            inv = 1.0 / ocol[k : k + 1, :]
            orow = jnp.where(at_col[:1], 1.0, other[k : k + 1, :]) * inv
            other = jnp.where(
                rows == k, orow, jnp.where(at_col, 0.0, other) - ocol * orow
            )
        work = jnp.concatenate([work[STEPS:], work[:STEPS]], axis=0)
        other = jnp.concatenate([other[STEPS:], other[:STEPS]], axis=0)
        return pltpu.roll(work, size - STEPS, 1), pltpu.roll(other, size - STEPS, 1)

    return lax.fori_loop(0, size // STEPS, block, (gram, top_t))


def split_factor(work, other):
    size = work.shape[0]
    rows = lax.broadcasted_iota(jnp.int32, (size, size), 0)
    cols = lax.broadcasted_iota(jnp.int32, (size, size), 1)
    linv = jnp.where(rows >= cols, work, 0.0)
    upper = jnp.where(rows < cols, work, jnp.where(rows == cols, 1.0 / jnp.where(rows == cols, work, 1.0), 0.0))
    coupling = lax.dot_general(
        other, upper, (((1,), (1,)), ((), ())), precision=lax.Precision.HIGHEST, preferred_element_type=jnp.float32
    )
    return linv, upper, coupling

MESH = pl.DeviceIdType.MESH
CHUNKS = 8
EARLY = 2
SLACK = 2
TILE = 256
GRANT = 24 * 1024 * 1024
F32 = jnp.float32


def exact_dot(left, right, dims):
    return lax.dot_general(
        left, right, (dims, ((), ())), precision=lax.Precision.HIGHEST, preferred_element_type=F32
    )


def split(value):
    high = value.astype(jnp.bfloat16)
    return high, (value - high.astype(F32)).astype(jnp.bfloat16)


def pair_dot(left, right, dims):
    (lh, ll), (rh, rl) = left, right

    def one(a, b):
        return lax.dot_general(a, b, (dims, ((), ())), preferred_element_type=F32)

    return one(lh, rh) + (one(lh, rl) + one(ll, rh))


def exchange_kernel(
    sizes, panel_ref, trail_ref, left_hi, left_lo, right_hi, right_lo, band_ref, t_buf,
    own_sem, t_sem, colp, colq, vcat, part, acc, got, prod, vec,
    gram_ref, rs_ref, both, small_ref, rs2_ref, both2,
    top_send, top_recv, rs_send, rs_recv, ag_send, ag_recv, rs2_send, rs2_recv, ag2_send, ag2_recv,
    pump_send, pump_recv, pump2_send, pump2_recv, red_send, red_recv, bit_send, bit_recv, back_send, back_recv,
):
    n, m, nx, blocks = sizes
    nz = n // nx
    rows, size = panel_ref.shape
    piece = size // n
    half = rows // 2
    chunk_rows = rows // CHUNKS
    me = lax.axis_index("prow")
    q = lax.axis_index("pcol")
    z, x = me // nx, me % nx
    bits = m.bit_length() - 1

    def flip(bit):
        step = 1 << bit
        return q + step - 2 * step * ((q // step) % 2)

    def peer(offset):
        return (me + offset) % n

    def remote(src, dst, send, recv, where):
        return pltpu.make_async_remote_copy(
            src_ref=src, dst_ref=dst, send_sem=send, recv_sem=recv, device_id=where, device_id_type=MESH
        )

    t_copy = pltpu.make_async_copy(trail_ref, t_buf, t_sem)
    t_copy.start()
    barrier = pltpu.get_barrier_semaphore()
    for offset in range(1, n):
        pl.semaphore_signal(barrier, inc=1, device_id={"prow": peer(offset)}, device_id_type=MESH)
    for bit in range(bits):
        pl.semaphore_signal(barrier, inc=1, device_id={"pcol": flip(bit)}, device_id_type=MESH)

    def place(k):
        b = q * blocks + k
        return b, z - b // nx, x - b % nx

    def fill(buf, source):
        for k in range(blocks):
            b, _, _ = place(k)

            @pl.when(me == b)
            def _():
                copy = pltpu.make_async_copy(source, buf.at[pl.ds(k * rows, rows)], own_sem)
                copy.start()
                copy.wait()

    fill(colp, panel_ref)
    pl.semaphore_wait(barrier, n - 1 + bits)

    def children(dz, dx):
        return (
            (jnp.logical_and(jnp.logical_and(dx == 0, dz >= 0), z < nz - 1), me + nx),
            (jnp.logical_and(jnp.logical_and(dx == 0, dz <= 0), z > 0), me - nx),
            (jnp.logical_and(dx >= 0, x < nx - 1), me + 1),
            (jnp.logical_and(dx <= 0, x > 0), me - 1),
        )

    def relays(dz, dx):
        flags = [has for has, _ in children(dz, dx)]
        return functools.reduce(jnp.logical_or, flags)

    def settle(buf, send, recv):
        for k in range(blocks):
            _, dz, dx = place(k)
            away = jnp.logical_or(dz != 0, dx != 0)

            @pl.when(jnp.logical_and(away, jnp.logical_not(relays(dz, dx))))
            def _():
                for c in range(CHUNKS):
                    part_of = buf.at[pl.ds(k * rows + c * chunk_rows, chunk_rows)]
                    remote(part_of, part_of, send.at[k, 0], recv.at[k, c], {"prow": peer(1)}).wait_recv()

    def pump(step, buf, send, recv):
        for k in range(blocks):
            _, dz, dx = place(k)
            far = jnp.where(dz < 0, -dz, dz) + jnp.where(dx < 0, -dx, dx)
            c = step - SLACK * far

            @pl.when(jnp.logical_and(c >= 0, c < CHUNKS))
            def _():
                part_of = buf.at[pl.ds(k * rows + c * chunk_rows, chunk_rows)]

                @pl.when(jnp.logical_and(far > 0, relays(dz, dx)))
                def _():
                    remote(part_of, part_of, send.at[k, 0], recv.at[k, c], {"prow": peer(1)}).wait_recv()

                for d, (has, to) in enumerate(children(dz, dx)):

                    @pl.when(has)
                    def _():
                        remote(part_of, part_of, send.at[k, d], recv.at[k, c], {"prow": to}).start()

    def drain(buf, send, recv):
        for k in range(blocks):
            _, dz, dx = place(k)
            whole = buf.at[pl.ds(k * rows, rows)]
            for d, (has, to) in enumerate(children(dz, dx)):

                @pl.when(has)
                def _():
                    remote(whole, whole, send.at[k, d], recv.at[k, 0], {"prow": peer(1)}).wait_send()

    total_steps = CHUNKS + SLACK * (nz - 1 + max(nx - 2, 0))

    def scatter(src, slots, send, recv):
        def copy(offset):
            to = peer(offset)
            return remote(
                src.at[pl.ds(to * piece, piece)], slots.at[offset], send.at[offset], recv.at[offset], {"prow": to}
            )

        return [copy(offset) for offset in range(1, n)]

    def spread(slots, send, recv):
        def copy(offset):
            return remote(slots.at[me], slots.at[me], send.at[offset], recv.at[offset], {"prow": peer(offset)})

        def arrive(offset):
            slot = slots.at[peer(n - offset)]
            return remote(slot, slot, send.at[offset], recv.at[offset], {"prow": peer(offset)})

        return [copy(o) for o in range(1, n)], [arrive(o) for o in range(1, n)]

    def collected(src, slots):
        value = src[pl.ds(me * piece, piece)]
        for offset in range(1, n):
            value = value + slots[offset]
        return value

    def top_copy(j):
        return remote(panel_ref.at[pl.ds(j * piece, piece)], both.at[j, 1], top_send.at[j], top_recv, {"prow": j})

    @pl.when(me == 0)
    def _():
        for j in range(1, n):
            top_copy(j).start()
        both[0, 1] = panel_ref[:piece]

    for step in range(EARLY):
        pump(step, colp, pump_send, pump_recv)
    gram_ref[...] = exact_dot(panel_ref[...], panel_ref[...], ((0,), (0,)))
    sends = scatter(gram_ref, rs_ref, rs_send, rs_recv)
    for copy in sends:
        copy.start()
    for step in range(EARLY, 2 * EARLY):
        pump(step, colp, pump_send, pump_recv)

    @pl.when(me > 0)
    def _():
        slot = both.at[me, 1]
        remote(slot, slot, top_send.at[0], top_recv, {"prow": peer(1)}).wait_recv()

    for copy in sends:
        copy.wait_recv()
    both[me, 0] = collected(gram_ref, rs_ref)
    sends2, arrivals = spread(both, ag_send, ag_recv)
    for copy in sends2:
        copy.start()
    for step in range(2 * EARLY, 3 * EARLY):
        pump(step, colp, pump_send, pump_recv)
    for copy in arrivals:
        copy.wait_recv()
    for copy in sends + sends2:
        copy.wait_send()

    @pl.when(me == 0)
    def _():
        for j in range(1, n):
            top_copy(j).wait_send()

    done = 3 * EARLY
    turns = size // STEPS
    work, other = factor_body(
        both[:, 0].reshape(size, size),
        both[:, 1].reshape(size, size).T,
        lambda turn: pump(done + turn, colp, pump_send, pump_recv),
    )
    for step in range(done + turns, total_steps):
        pump(step, colp, pump_send, pump_recv)
    settle(colp, pump_send, pump_recv)
    linv, upper, coupling = split_factor(work, other)
    band_ref[...] = -upper
    linv_pair = split(linv)

    def unit(start):
        r = lax.broadcasted_iota(jnp.int32, (TILE, size), 0) + start
        return jnp.where(r == lax.broadcasted_iota(jnp.int32, (TILE, size), 1), 1.0, 0.0)

    def col_vectors(i, carry):
        at = pl.ds(pl.multiple_of(i * TILE, TILE), TILE)
        value = pair_dot(split(colp[at]), linv_pair, ((1,), (1,))) + unit(q * blocks * rows + i * TILE)
        high, low = split(value)
        vcat[at, :size] = high
        vcat[at, size:] = low
        right_hi[at, size:] = high
        right_lo[at, size:] = low
        return carry

    lax.fori_loop(0, blocks * rows // TILE, col_vectors, 0)
    t_copy.wait()

    h = q % 2
    per_half = half // TILE
    mate = {"pcol": flip(0)}

    def half_at(side, i):
        return pl.ds(pl.multiple_of(side * half + i * TILE, TILE), TILE)

    def tile_of(i):
        return pl.ds(pl.multiple_of(i * TILE, TILE), TILE)

    def red_copy(i):
        return remote(part.at[half_at(1 - h, i)], got.at[0, tile_of(i)], red_send.at[i], red_recv.at[i], mate)

    def times(side):
        def body(i, carry):
            at = half_at(side, i)
            high, low = split(t_buf[at])
            wide = lax.dot_general(high, vcat[...], (((1,), (0,)), ((), ())), preferred_element_type=F32)
            rest = lax.dot_general(low, vcat[:, :size], (((1,), (0,)), ((), ())), preferred_element_type=F32)
            part[at] = wide[:, :size] + (wide[:, size:] + rest)

            @pl.when(side != h)
            def _():
                red_copy(i).start()

            return carry

        lax.fori_loop(0, per_half, body, 0)

    times(1 - h)
    times(h)

    def bit_copy(bit, i):
        return remote(
            acc.at[bit, tile_of(i)], got.at[bit, tile_of(i)], bit_send.at[bit, i], bit_recv.at[bit, i],
            {"pcol": flip(bit)},
        )

    def back_copy(i, side):
        at = half_at(side, i)
        return remote(prod.at[at], prod.at[at], back_send.at[i], back_recv.at[i], mate)

    for i in range(per_half):
        red_copy(i).wait_recv()
        value = part[half_at(h, i)] + got[0, tile_of(i)]
        if bits > 1:
            acc[1, tile_of(i)] = value
            bit_copy(1, i).start()
        else:
            prod[half_at(h, i)] = value
            back_copy(i, h).start()

    def row_vectors(i, carry):
        at = tile_of(i)
        value = pair_dot(split(panel_ref[at]), linv_pair, ((1,), (1,))) + unit(me * rows + i * TILE)
        vec[at] = value
        left_hi[at, :size], left_lo[at, :size] = split(value)
        return carry

    lax.fori_loop(0, rows // TILE, row_vectors, 0)
    for bit in range(1, bits):
        for i in range(per_half):
            bit_copy(bit, i).wait_recv()
            value = acc[bit, tile_of(i)] + got[bit, tile_of(i)]
            if bit + 1 < bits:
                acc[bit + 1, tile_of(i)] = value
                bit_copy(bit + 1, i).start()
            else:
                prod[half_at(h, i)] = value
                back_copy(i, h).start()
    for i in range(per_half):
        back_copy(i, 1 - h).wait_recv()
    fill(colq, prod)
    for step in range(EARLY):
        pump(step, colq, pump2_send, pump2_recv)
    small_ref[...] = exact_dot(vec[...], prod[...], ((0,), (0,)))
    sends = scatter(small_ref, rs2_ref, rs2_send, rs2_recv)
    for copy in sends:
        copy.start()
    for step in range(EARLY, 2 * EARLY):
        pump(step, colq, pump2_send, pump2_recv)
    for copy in sends:
        copy.wait_recv()
    both2[me] = collected(small_ref, rs2_ref)
    sends2, arrivals = spread(both2, ag2_send, ag2_recv)
    for copy in sends2:
        copy.start()
    for step in range(2 * EARLY, 3 * EARLY):
        pump(step, colq, pump2_send, pump2_recv)

    def rest(step, carry):
        pump(step, colq, pump2_send, pump2_recv)
        return carry

    lax.fori_loop(done, total_steps, rest, 0)
    for copy in arrivals:
        copy.wait_recv()
    inner = exact_dot(both2[...].reshape(size, size), coupling, ((1,), (0,)))
    small = exact_dot(coupling, inner, ((0,), (0,)))
    coupling_pair = split(coupling)
    small_pair = split(-0.5 * small)

    def row_update(i, carry):
        at = tile_of(i)
        value = pair_dot(split(prod[at]), coupling_pair, ((1,), (0,)))
        value = value + pair_dot((left_hi[at, :size], left_lo[at, :size]), small_pair, ((1,), (0,)))
        left_hi[at, size:], left_lo[at, size:] = split(value)
        return carry

    lax.fori_loop(0, rows // TILE, row_update, 0)

    settle(colq, pump2_send, pump2_recv)

    def col_update(i, carry):
        at = tile_of(i)
        value = pair_dot(split(colq[at]), coupling_pair, ((1,), (0,)))
        value = value + pair_dot((vcat[at, :size], vcat[at, size:]), small_pair, ((1,), (0,)))
        right_hi[at, :size], right_lo[at, :size] = split(value)
        return carry

    lax.fori_loop(0, blocks * rows // TILE, col_update, 0)
    for copy in sends + sends2:
        copy.wait_send()
    for i in range(per_half):
        red_copy(i).wait_send()
        back_copy(i, h).wait_send()
        for bit in range(1, bits):
            bit_copy(bit, i).wait_send()
    drain(colp, pump_send, pump_recv)
    drain(colq, pump2_send, pump2_recv)


def exchange(panel, trailing, n, m, nx):
    rows, size = panel.shape
    cols = trailing.shape[1]
    blocks = cols // rows
    piece, half = size // n, rows // 2
    bits = max(m.bit_length() - 1, 2)
    dma = pltpu.SemaphoreType.DMA
    vmem = pl.BlockSpec(memory_space=pltpu.VMEM)
    narrow = jnp.bfloat16
    return pl.pallas_call(
        functools.partial(exchange_kernel, (n, m, nx, blocks)),
        out_shape=[
            jax.ShapeDtypeStruct((rows, 2 * size), narrow),
            jax.ShapeDtypeStruct((rows, 2 * size), narrow),
            jax.ShapeDtypeStruct((cols, 2 * size), narrow),
            jax.ShapeDtypeStruct((cols, 2 * size), narrow),
            jax.ShapeDtypeStruct((size, size), F32),
            jax.ShapeDtypeStruct((rows, cols), F32),
        ],
        in_specs=[vmem, pl.BlockSpec(memory_space=pltpu.HBM)],
        out_specs=[vmem] * 6,
        scratch_shapes=[
            dma,
            dma,
            pltpu.VMEM((cols, size), F32),
            pltpu.VMEM((cols, size), F32),
            pltpu.VMEM((cols, 2 * size), narrow),
            pltpu.VMEM((rows, size), F32),
            pltpu.VMEM((bits, half, size), F32),
            pltpu.VMEM((bits, half, size), F32),
            pltpu.VMEM((rows, size), F32),
            pltpu.VMEM((rows, size), F32),
            pltpu.VMEM((size, size), F32),
            pltpu.VMEM((n, piece, size), F32),
            pltpu.VMEM((n, 2, piece, size), F32),
            pltpu.VMEM((size, size), F32),
            pltpu.VMEM((n, piece, size), F32),
            pltpu.VMEM((n, piece, size), F32),
            dma((n,)), dma,
            dma((n,)), dma((n,)), dma((n,)), dma((n,)),
            dma((n,)), dma((n,)), dma((n,)), dma((n,)),
            dma((blocks, 4)), dma((blocks, CHUNKS)),
            dma((blocks, 4)), dma((blocks, CHUNKS)),
            dma((half // TILE,)), dma((half // TILE,)),
            dma((bits, half // TILE)), dma((bits, half // TILE)),
            dma((half // TILE,)), dma((half // TILE,)),
        ],
        compiler_params=pltpu.CompilerParams(
            collective_id=0, has_side_effects=True, vmem_limit_bytes=40 * 1024 * 1024
        ),
        name="exchange",
    )(panel, trailing)


def finish_kernel(t_ref, lh, ll, rh, rl, band_ref, out_ref, band_out):
    dims = (((1,), (1,)), ((), ()))
    wide = out_ref.shape[1]
    at = pl.ds(pl.multiple_of(pl.program_id(0) * wide, wide), wide)

    def one(a, b):
        return lax.dot_general(a, b, dims, preferred_element_type=F32)

    out_ref[...] = t_ref[:, at] - (
        one(lh[...], rh[at]) + (one(lh[...], rl[at]) + one(ll[...], rh[at]))
    )

    @pl.when(pl.program_id(0) == 0)
    def _():
        band_out[...] = band_ref[...]


def finish(trailing, lh, ll, rh, rl, band):
    rows, cols = trailing.shape
    tile = 2 * TILE
    whole = pl.BlockSpec(memory_space=pltpu.VMEM)
    return pl.pallas_call(
        finish_kernel,
        grid=(cols // tile,),
        out_shape=[jax.ShapeDtypeStruct((rows, cols), F32), jax.ShapeDtypeStruct(band.shape, F32)],
        in_specs=[whole] * 6,
        out_specs=[pl.BlockSpec((rows, tile), lambda i: (0, i)), whole],
        compiler_params=pltpu.CompilerParams(vmem_limit_bytes=GRANT),
        name="finish",
    )(trailing, lh, ll, rh, rl, band)


def shards(n, m, nx, panel, trailing):
    lh, ll, rh, rl, band, held = exchange(panel, trailing, n, m, nx)
    return tuple(finish(held, lh, ll, rh, rl, band))


def solution(mesh):
    placed = (P("prow", None), P("prow", "pcol"))
    n, m = mesh.shape["prow"], mesh.shape["pcol"]
    column = [getattr(d, "coords", None) for d in mesh.devices[:, 0]]
    nx = 2 if None in column else len({c[0] for c in column})
    return jax.shard_map(
        functools.partial(shards, n, m, nx),
        mesh=mesh,
        in_specs=placed,
        out_specs=(P("prow", "pcol"), P()),
        check_vma=False,
    )
```

profile of v0, /device:TPU:5, one launch (start us, length us, event | category | flops | bytes accessed | tf_op | source)
XLA Modules:
  0.0 77.0 jit_solution(16827127135020541742)
XLA Ops:
  0.6 0.0 copy-start
  0.6 1.0 %copy-done = f32[1024,128]{1,0:T(8,128)S(1)} copy-done((f32[1024,128]{1,0:T(8,128)S(1)}, f32[1024,128]{1,0:T(8,128)}, u32[]{:S(2)}) %copy-start) | copy-done | bytes 524312
  1.7 69.6 %exchange.1 = (bf16[1024,256]{1,0:T(8,128)(2,1)S(1)}, bf16[1024,256]{1,0:T(8,128)(2,1)S(1)}, bf16[2048,256]{1,0:T(8,128)(2,1)S(1)}, bf16[2048,256]{1,0:T(8,128)(...) custom-call(f32[1024,128]{1,0:T(8,128)S(1)} %copy-done, f32[1024,2048]{1,0:T(8,128)} %trail_ref.1), custom_call_target="tpu_custom_call" | custom-call | tf_op jit(solution)/shard_map/exchange/pallas_call | solution.py:435
  71.3 5.7 %finish.1 = (f32[1024,2048]{1,0:T(8,128)}, f32[128,128]{1,0:T(8,128)}) custom-call(f32[1024,2048]{1,0:T(8,128)S(1)} %get-tuple-element.8.t_ref, bf16[1024,256]{1,0:T(8,128)(2,1)S(1)} %get-tuple-element.9.lh, bf16[1024,256]{1,0:T(8,128)(2,1)S(1)} %get-tuple-element.10.ll, bf16[2048,256]{1,0:T(8,128)(2,1)S(1)} %get-tuple-element.11.rh, ...), custom_call_target="tpu_custom_call" | custom-call | tf_op jit(solution)/shard_map/finish/pallas_call | solution.py:501
Async XLA Ops:
  0.6 1.0 %copy-start = (f32[1024,128]{1,0:T(8,128)S(1)}, f32[1024,128]{1,0:T(8,128)}, u32[]{:S(2)}) copy-start(f32[1024,128]{1,0:T(8,128)} %panel_ref.1) | copy-start | bytes 1572868
where the time goes:
time: 77.2 us; the launch traced here: 77 us
  Pallas kernels  75.3 us (98%)
  local copies, waits for them, and re-layouts  1.03 us (1%)
    pallas_call x1, Pallas kernels, exchange(): pl.pallas_call(functools.partial(exchange_kernel, (n, m, nx, blocks)), ou...  69.6 us
    pallas_call x1, Pallas kernels, finish(): pl.pallas_call(finish_kernel, grid=(cols // tile,), out_shape=[jax.ShapeD...  5.71 us

commit v1 on v0

--- a/solution.py
+++ b/solution.py
@@ -17,9 +17,10 @@
 
     def block(turn, carry):
         work, other = carry
-        between(turn)
         live = size - turn * STEPS
         for k in range(STEPS):
+            if k % (STEPS // 2) == 0:
+                between(2 * turn + 2 * k // STEPS)
             at_col = cols == k
             below = jnp.logical_and(rows > k, rows < live)
             col = jnp.broadcast_to(work[:, k : k + 1], (size, size))
@@ -56,10 +57,11 @@
     return linv, upper, coupling
 
 MESH = pl.DeviceIdType.MESH
-CHUNKS = 8
-EARLY = 2
+CHUNKS = 16
+EARLY = (2, 5, 5)
 SLACK = 2
 TILE = 256
+PAIR = 4
 GRANT = 24 * 1024 * 1024
 F32 = jnp.float32
 
@@ -85,10 +87,10 @@
 
 
 def exchange_kernel(
-    sizes, panel_ref, trail_ref, left_hi, left_lo, right_hi, right_lo, band_ref, t_buf,
-    own_sem, t_sem, colp, colq, vcat, part, acc, got, prod, vec,
-    gram_ref, rs_ref, both, small_ref, rs2_ref, both2,
-    top_send, top_recv, rs_send, rs_recv, ag_send, ag_recv, rs2_send, rs2_recv, ag2_send, ag2_recv,
+    sizes, panel_hbm, trail_ref, left_hi, left_lo, right_hi, right_lo, band_ref, t_buf,
+    panel_ref, p_sem, own_sem, t_sem, colp, colq, vcat, part, acc, got, prod, vec,
+    gram_ref, rs_ref, both, small_ref, rs2_ref, pc_ref, both2,
+    top_send, top_recv, rs_send, rs_recv, ag_send, ag_recv, rs2_send, rs2_recv, ag2_send, ag2_recv, pc_send, pc_recv,
     pump_send, pump_recv, pump2_send, pump2_recv, red_send, red_recv, bit_send, bit_recv, back_send, back_recv,
 ):
     n, m, nx, blocks = sizes
@@ -115,29 +117,38 @@
         )
 
     t_copy = pltpu.make_async_copy(trail_ref, t_buf, t_sem)
+    p_copy = pltpu.make_async_copy(panel_hbm, panel_ref, p_sem)
+    p_copy.start()
     t_copy.start()
     barrier = pltpu.get_barrier_semaphore()
     for offset in range(1, n):
         pl.semaphore_signal(barrier, inc=1, device_id={"prow": peer(offset)}, device_id_type=MESH)
-    for bit in range(bits):
-        pl.semaphore_signal(barrier, inc=1, device_id={"pcol": flip(bit)}, device_id_type=MESH)
+    for offset in range(1, m):
+        pl.semaphore_signal(barrier, inc=1, device_id={"pcol": (q + offset) % m}, device_id_type=MESH)
 
     def place(k):
         b = q * blocks + k
         return b, z - b // nx, x - b % nx
 
-    def fill(buf, source):
+    def filled(buf, source):
+        copies = []
         for k in range(blocks):
             b, _, _ = place(k)
-
-            @pl.when(me == b)
-            def _():
-                copy = pltpu.make_async_copy(source, buf.at[pl.ds(k * rows, rows)], own_sem)
-                copy.start()
-                copy.wait()
-
+            copies.append((me == b, pltpu.make_async_copy(source, buf.at[pl.ds(k * rows, rows)], own_sem)))
+        return copies
+
+    def fill(buf, source):
+        for mine, copy in filled(buf, source):
+            pl.when(mine)(copy.start)
+
+    def fill_wait(buf, source):
+        for mine, copy in filled(buf, source):
+            pl.when(mine)(copy.wait)
+
+    p_copy.wait()
     fill(colp, panel_ref)
-    pl.semaphore_wait(barrier, n - 1 + bits)
+    fill_wait(colp, panel_ref)
+    pl.semaphore_wait(barrier, n - 1 + m - 1)
 
     def children(dz, dx):
         return (
@@ -151,18 +162,27 @@
         flags = [has for has, _ in children(dz, dx)]
         return functools.reduce(jnp.logical_or, flags)
 
-    def settle(buf, send, recv):
+    def in_order(k, c):
+        return pl.multiple_of(c * chunk_rows, chunk_rows)
+
+    def paired(k, c):
+        first = place(k)[0] // blocks % 2
+        side = (first + c % PAIR // (PAIR // 2)) % 2
+        at = side * half + c // PAIR * (PAIR // 2) * chunk_rows + c % (PAIR // 2) * chunk_rows
+        return pl.multiple_of(at, chunk_rows)
+
+    def settle(buf, send, recv, where, span):
         for k in range(blocks):
             _, dz, dx = place(k)
             away = jnp.logical_or(dz != 0, dx != 0)
 
             @pl.when(jnp.logical_and(away, jnp.logical_not(relays(dz, dx))))
             def _():
-                for c in range(CHUNKS):
-                    part_of = buf.at[pl.ds(k * rows + c * chunk_rows, chunk_rows)]
+                for c in span:
+                    part_of = buf.at[pl.ds(k * rows + where(k, c), chunk_rows)]
                     remote(part_of, part_of, send.at[k, 0], recv.at[k, c], {"prow": peer(1)}).wait_recv()
 
-    def pump(step, buf, send, recv):
+    def pump(step, buf, source, send, recv, where):
         for k in range(blocks):
             _, dz, dx = place(k)
             far = jnp.where(dz < 0, -dz, dz) + jnp.where(dx < 0, -dx, dx)
@@ -170,7 +190,7 @@
 
             @pl.when(jnp.logical_and(c >= 0, c < CHUNKS))
             def _():
-                part_of = buf.at[pl.ds(k * rows + c * chunk_rows, chunk_rows)]
+                part_of = buf.at[pl.ds(k * rows + where(k, c), chunk_rows)]
 
                 @pl.when(jnp.logical_and(far > 0, relays(dz, dx)))
                 def _():
@@ -178,9 +198,20 @@
 
                 for d, (has, to) in enumerate(children(dz, dx)):
 
-                    @pl.when(has)
+                    @pl.when(jnp.logical_and(has, far > 0))
                     def _():
                         remote(part_of, part_of, send.at[k, d], recv.at[k, c], {"prow": to}).start()
+
+                    @pl.when(jnp.logical_and(has, far == 0))
+                    def _():
+                        own = source.at[pl.ds(where(k, c), chunk_rows)]
+                        remote(own, part_of, send.at[k, d], recv.at[k, c], {"prow": to}).start()
+
+    def pump_p(step):
+        pump(step, colp, panel_ref, pump_send, pump_recv, in_order)
+
+    def pump_q(step):
+        pump(step, colq, prod, pump2_send, pump2_recv, paired)
 
     def drain(buf, send, recv):
         for k in range(blocks):
@@ -228,14 +259,14 @@
             top_copy(j).start()
         both[0, 1] = panel_ref[:piece]
 
-    for step in range(EARLY):
-        pump(step, colp, pump_send, pump_recv)
+    for step in range(EARLY[0]):
+        pump_p(step)
     gram_ref[...] = exact_dot(panel_ref[...], panel_ref[...], ((0,), (0,)))
     sends = scatter(gram_ref, rs_ref, rs_send, rs_recv)
     for copy in sends:
         copy.start()
-    for step in range(EARLY, 2 * EARLY):
-        pump(step, colp, pump_send, pump_recv)
+    for step in range(EARLY[0], sum(EARLY[:2])):
+        pump_p(step)
 
     @pl.when(me > 0)
     def _():
@@ -248,8 +279,8 @@
     sends2, arrivals = spread(both, ag_send, ag_recv)
     for copy in sends2:
         copy.start()
-    for step in range(2 * EARLY, 3 * EARLY):
-        pump(step, colp, pump_send, pump_recv)
+    for step in range(sum(EARLY[:2]), sum(EARLY)):
+        pump_p(step)
     for copy in arrivals:
         copy.wait_recv()
     for copy in sends + sends2:
@@ -260,16 +291,16 @@
         for j in range(1, n):
             top_copy(j).wait_send()
 
-    done = 3 * EARLY
-    turns = size // STEPS
+    done = sum(EARLY)
+    turns = 2 * (size // STEPS)
     work, other = factor_body(
         both[:, 0].reshape(size, size),
         both[:, 1].reshape(size, size).T,
-        lambda turn: pump(done + turn, colp, pump_send, pump_recv),
+        lambda turn: pump_p(done + turn),
     )
     for step in range(done + turns, total_steps):
-        pump(step, colp, pump_send, pump_recv)
-    settle(colp, pump_send, pump_recv)
+        pump_p(step)
+    settle(colp, pump_send, pump_recv, in_order, range(CHUNKS))
     linv, upper, coupling = split_factor(work, other)
     band_ref[...] = -upper
     linv_pair = split(linv)
@@ -323,25 +354,32 @@
     times(1 - h)
     times(h)
 
+    small_rows = PAIR // 2 * chunk_rows
+    tiles = half // small_rows
+    last = bits - 1
+
+    def small_at(i):
+        return pl.ds(i * small_rows, small_rows)
+
+    def side_at(side, i):
+        return pl.ds(pl.multiple_of(side * half + i * small_rows, small_rows), small_rows)
+
     def bit_copy(bit, i):
         return remote(
-            acc.at[bit, tile_of(i)], got.at[bit, tile_of(i)], bit_send.at[bit, i], bit_recv.at[bit, i],
+            acc.at[bit, small_at(i)], got.at[bit, small_at(i)], bit_send.at[bit, i], bit_recv.at[bit, i],
             {"pcol": flip(bit)},
         )
 
     def back_copy(i, side):
-        at = half_at(side, i)
+        at = side_at(side, i)
         return remote(prod.at[at], prod.at[at], back_send.at[i], back_recv.at[i], mate)
 
     for i in range(per_half):
         red_copy(i).wait_recv()
-        value = part[half_at(h, i)] + got[0, tile_of(i)]
         if bits > 1:
-            acc[1, tile_of(i)] = value
-            bit_copy(1, i).start()
-        else:
-            prod[half_at(h, i)] = value
-            back_copy(i, h).start()
+            acc[1, tile_of(i)] = part[half_at(h, i)] + got[0, tile_of(i)]
+            for j in range(i * TILE // small_rows, (i + 1) * TILE // small_rows):
+                bit_copy(1, j).start()
 
     def row_vectors(i, carry):
         at = tile_of(i)
@@ -351,41 +389,60 @@
         return carry
 
     lax.fori_loop(0, rows // TILE, row_vectors, 0)
-    for bit in range(1, bits):
-        for i in range(per_half):
-            bit_copy(bit, i).wait_recv()
-            value = acc[bit, tile_of(i)] + got[bit, tile_of(i)]
-            if bit + 1 < bits:
-                acc[bit + 1, tile_of(i)] = value
-                bit_copy(bit + 1, i).start()
-            else:
-                prod[half_at(h, i)] = value
-                back_copy(i, h).start()
-    for i in range(per_half):
-        back_copy(i, 1 - h).wait_recv()
-    fill(colq, prod)
-    for step in range(EARLY):
-        pump(step, colq, pump2_send, pump2_recv)
-    small_ref[...] = exact_dot(vec[...], prod[...], ((0,), (0,)))
+    small_ref[...] = exact_dot(vec[...], part[...], ((0,), (0,)))
     sends = scatter(small_ref, rs2_ref, rs2_send, rs2_recv)
     for copy in sends:
         copy.start()
-    for step in range(EARLY, 2 * EARLY):
-        pump(step, colq, pump2_send, pump2_recv)
-    for copy in sends:
-        copy.wait_recv()
-    both2[me] = collected(small_ref, rs2_ref)
+
+    for bit in range(1, last):
+        for i in range(tiles):
+            bit_copy(bit, i).wait_recv()
+            acc[bit + 1, small_at(i)] = acc[bit, small_at(i)] + got[bit, small_at(i)]
+            bit_copy(bit + 1, i).start()
+
+    def across(offset):
+        to = (q + offset) % m
+        return remote(pc_ref.at[q], pc_ref.at[q], pc_send.at[offset], pc_recv.at[offset], {"pcol": to})
+
+    def came(offset):
+        slot = pc_ref.at[(q - offset + m) % m]
+        return remote(slot, slot, pc_send.at[offset], pc_recv.at[offset], {"pcol": (q + offset) % m})
+
+    crossing = [across(o) for o in range(1, m)]
+    for i in range(tiles + 1):
+        if i < tiles:
+            if bits > 1:
+                bit_copy(last, i).wait_recv()
+                prod[side_at(h, i)] = acc[last, small_at(i)] + got[last, small_at(i)]
+            else:
+                prod[side_at(h, i)] = part[side_at(h, i)] + got[0, small_at(i)]
+            back_copy(i, h).start()
+        if i == tiles // 2:
+            for copy in sends:
+                copy.wait_recv()
+            pc_ref[q] = collected(small_ref, rs2_ref)
+            for copy in crossing:
+                copy.start()
+        if i > 0:
+            back_copy(i - 1, 1 - h).wait_recv()
+            for step in range(PAIR * (i - 1), PAIR * i):
+                pump_q(step)
+    fill(colq, prod)
+    for o in range(1, m):
+        came(o).wait_recv()
+    value = pc_ref[0]
+    for j in range(1, m):
+        value = value + pc_ref[j]
+    both2[me] = value
     sends2, arrivals = spread(both2, ag2_send, ag2_recv)
     for copy in sends2:
         copy.start()
-    for step in range(2 * EARLY, 3 * EARLY):
-        pump(step, colq, pump2_send, pump2_recv)
 
     def rest(step, carry):
-        pump(step, colq, pump2_send, pump2_recv)
+        pump_q(step)
         return carry
 
-    lax.fori_loop(done, total_steps, rest, 0)
+    lax.fori_loop(CHUNKS, total_steps, rest, 0)
     for copy in arrivals:
         copy.wait_recv()
     inner = exact_dot(both2[...].reshape(size, size), coupling, ((1,), (0,)))
@@ -401,21 +458,26 @@
         return carry
 
     lax.fori_loop(0, rows // TILE, row_update, 0)
-
-    settle(colq, pump2_send, pump2_recv)
-
-    def col_update(i, carry):
-        at = tile_of(i)
-        value = pair_dot(split(colq[at]), coupling_pair, ((1,), (0,)))
-        value = value + pair_dot((vcat[at, :size], vcat[at, size:]), small_pair, ((1,), (0,)))
-        right_hi[at, :size], right_lo[at, :size] = split(value)
-        return carry
-
-    lax.fori_loop(0, blocks * rows // TILE, col_update, 0)
+    fill_wait(colq, prod)
+
+    for j in range(tiles):
+        settle(colq, pump2_send, pump2_recv, paired, range(PAIR * j, PAIR * (j + 1)))
+
+        def col_update(i, carry):
+            at = pl.ds(pl.multiple_of(i * half + j * small_rows, small_rows), small_rows)
+            value = pair_dot(split(colq[at]), coupling_pair, ((1,), (0,)))
+            value = value + pair_dot((vcat[at, :size], vcat[at, size:]), small_pair, ((1,), (0,)))
+            right_hi[at, :size], right_lo[at, :size] = split(value)
+            return carry
+
+        lax.fori_loop(0, 2 * blocks, col_update, 0)
+    for copy in crossing:
+        copy.wait_send()
     for copy in sends + sends2:
         copy.wait_send()
     for i in range(per_half):
         red_copy(i).wait_send()
+    for i in range(tiles):
         back_copy(i, h).wait_send()
         for bit in range(1, bits):
             bit_copy(bit, i).wait_send()
@@ -429,6 +491,7 @@
     blocks = cols // rows
     piece, half = size // n, rows // 2
     bits = max(m.bit_length() - 1, 2)
+    tiles = half // (PAIR // 2 * (rows // CHUNKS))
     dma = pltpu.SemaphoreType.DMA
     vmem = pl.BlockSpec(memory_space=pltpu.VMEM)
     narrow = jnp.bfloat16
@@ -442,9 +505,11 @@
             jax.ShapeDtypeStruct((size, size), F32),
             jax.ShapeDtypeStruct((rows, cols), F32),
         ],
-        in_specs=[vmem, pl.BlockSpec(memory_space=pltpu.HBM)],
+        in_specs=[pl.BlockSpec(memory_space=pltpu.HBM)] * 2,
         out_specs=[vmem] * 6,
         scratch_shapes=[
+            pltpu.VMEM((rows, size), F32),
+            dma,
             dma,
             dma,
             pltpu.VMEM((cols, size), F32),
@@ -460,15 +525,17 @@
             pltpu.VMEM((n, 2, piece, size), F32),
             pltpu.VMEM((size, size), F32),
             pltpu.VMEM((n, piece, size), F32),
+            pltpu.VMEM((m, piece, size), F32),
             pltpu.VMEM((n, piece, size), F32),
             dma((n,)), dma,
             dma((n,)), dma((n,)), dma((n,)), dma((n,)),
             dma((n,)), dma((n,)), dma((n,)), dma((n,)),
+            dma((m,)), dma((m,)),
             dma((blocks, 4)), dma((blocks, CHUNKS)),
             dma((blocks, 4)), dma((blocks, CHUNKS)),
             dma((half // TILE,)), dma((half // TILE,)),
-            dma((bits, half // TILE)), dma((bits, half // TILE)),
-            dma((half // TILE,)), dma((half // TILE,)),
+            dma((bits, tiles)), dma((bits, tiles)),
+            dma((tiles,)), dma((tiles,)),
         ],
         compiler_params=pltpu.CompilerParams(
             collective_id=0, has_side_effects=True, vmem_limit_bytes=40 * 1024 * 1024

time: 77.2 us -> 79.1 us (1.025)
  the two profiles are of different devices: /device:TPU:5 before, /device:TPU:0 now
where the time goes in v1:
time: 79.1 us; the launch traced here: 78.9 us
  Pallas kernels  77.2 us (98%)
  local copies, waits for them, and re-layouts  1.03 us (1%)
    pallas_call x1, Pallas kernels, exchange(): pl.pallas_call(functools.partial(exchange_kernel, (n, m, nx, blocks)), ou...  71.5 us
    pallas_call x1, Pallas kernels, finish(): pl.pallas_call(finish_kernel, grid=(cols // tile,), out_shape=[jax.ShapeD...  5.71 us

profile of v1, /device:TPU:0, one launch (start us, length us, event | category | flops | bytes accessed | tf_op | source)
XLA Modules:
  0.0 78.9 jit_solution(5704035225635675592)
XLA Ops:
  0.6 0.0 copy-start
  0.6 1.0 %copy-done = f32[1024,128]{1,0:T(8,128)S(1)} copy-done((f32[1024,128]{1,0:T(8,128)S(1)}, f32[1024,128]{1,0:T(8,128)}, u32[]{:S(2)}) %copy-start) | copy-done | bytes 524312
  1.7 71.5 %exchange.1 = (bf16[1024,256]{1,0:T(8,128)(2,1)S(1)}, bf16[1024,256]{1,0:T(8,128)(2,1)S(1)}, bf16[2048,256]{1,0:T(8,128)(2,1)S(1)}, bf16[2048,256]{1,0:T(8,128)(...) custom-call(f32[1024,128]{1,0:T(8,128)S(1)} %copy-done, f32[1024,2048]{1,0:T(8,128)} %trail_ref.1), custom_call_target="tpu_custom_call" | custom-call | tf_op jit(solution)/shard_map/exchange/pallas_call | solution.py:498
  73.2 5.7 %finish.1 = (f32[1024,2048]{1,0:T(8,128)}, f32[128,128]{1,0:T(8,128)}) custom-call(f32[1024,2048]{1,0:T(8,128)S(1)} %get-tuple-element.8.t_ref, bf16[1024,256]{1,0:T(8,128)(2,1)S(1)} %get-tuple-element.9.lh, bf16[1024,256]{1,0:T(8,128)(2,1)S(1)} %get-tuple-element.10.ll, bf16[2048,256]{1,0:T(8,128)(2,1)S(1)} %get-tuple-element.11.rh, ...), custom_call_target="tpu_custom_call" | custom-call | tf_op jit(solution)/shard_map/finish/pallas_call | solution.py:568
Async XLA Ops:
  0.6 1.0 %copy-start = (f32[1024,128]{1,0:T(8,128)S(1)}, f32[1024,128]{1,0:T(8,128)}, u32[]{:S(2)}) copy-start(f32[1024,128]{1,0:T(8,128)} %panel_hbm.1) | copy-start | bytes 1572868

commit v2 on v1

--- a/solution.py
+++ b/solution.py
@@ -58,8 +58,8 @@
 
 MESH = pl.DeviceIdType.MESH
 CHUNKS = 16
-EARLY = (2, 5, 5)
-SLACK = 2
+EARLY = (4, 4, 4)
+SLACK = (4, 4)
 TILE = 256
 PAIR = 4
 GRANT = 24 * 1024 * 1024
@@ -87,8 +87,8 @@
 
 
 def exchange_kernel(
-    sizes, panel_hbm, trail_ref, left_hi, left_lo, right_hi, right_lo, band_ref, t_buf,
-    panel_ref, p_sem, own_sem, t_sem, colp, colq, vcat, part, acc, got, prod, vec,
+    sizes, panel_ref, trail_ref, left_hi, left_lo, right_hi, right_lo, band_ref, t_buf,
+    own_sem, t_sem, colp, colq, vcat, part, acc, got, prod, vec,
     gram_ref, rs_ref, both, small_ref, rs2_ref, pc_ref, both2,
     top_send, top_recv, rs_send, rs_recv, ag_send, ag_recv, rs2_send, rs2_recv, ag2_send, ag2_recv, pc_send, pc_recv,
     pump_send, pump_recv, pump2_send, pump2_recv, red_send, red_recv, bit_send, bit_recv, back_send, back_recv,
@@ -117,8 +117,6 @@
         )
 
     t_copy = pltpu.make_async_copy(trail_ref, t_buf, t_sem)
-    p_copy = pltpu.make_async_copy(panel_hbm, panel_ref, p_sem)
-    p_copy.start()
     t_copy.start()
     barrier = pltpu.get_barrier_semaphore()
     for offset in range(1, n):
@@ -145,8 +143,8 @@
         for mine, copy in filled(buf, source):
             pl.when(mine)(copy.wait)
 
-    p_copy.wait()
     fill(colp, panel_ref)
+    gram_ref[...] = exact_dot(panel_ref[...], panel_ref[...], ((0,), (0,)))
     fill_wait(colp, panel_ref)
     pl.semaphore_wait(barrier, n - 1 + m - 1)
 
@@ -182,11 +180,11 @@
                     part_of = buf.at[pl.ds(k * rows + where(k, c), chunk_rows)]
                     remote(part_of, part_of, send.at[k, 0], recv.at[k, c], {"prow": peer(1)}).wait_recv()
 
-    def pump(step, buf, source, send, recv, where):
+    def pump(step, buf, source, send, recv, where, slack):
         for k in range(blocks):
             _, dz, dx = place(k)
             far = jnp.where(dz < 0, -dz, dz) + jnp.where(dx < 0, -dx, dx)
-            c = step - SLACK * far
+            c = step - slack * far
 
             @pl.when(jnp.logical_and(c >= 0, c < CHUNKS))
             def _():
@@ -208,10 +206,10 @@
                         remote(own, part_of, send.at[k, d], recv.at[k, c], {"prow": to}).start()
 
     def pump_p(step):
-        pump(step, colp, panel_ref, pump_send, pump_recv, in_order)
+        pump(step, colp, panel_ref, pump_send, pump_recv, in_order, SLACK[0])
 
     def pump_q(step):
-        pump(step, colq, prod, pump2_send, pump2_recv, paired)
+        pump(step, colq, prod, pump2_send, pump2_recv, paired, SLACK[1])
 
     def drain(buf, send, recv):
         for k in range(blocks):
@@ -223,7 +221,7 @@
                 def _():
                     remote(whole, whole, send.at[k, d], recv.at[k, 0], {"prow": peer(1)}).wait_send()
 
-    total_steps = CHUNKS + SLACK * (nz - 1 + max(nx - 2, 0))
+    steps_p, steps_q = [CHUNKS + slack * (nz - 1 + max(nx - 1, 0)) for slack in SLACK]
 
     def scatter(src, slots, send, recv):
         def copy(offset):
@@ -261,7 +259,6 @@
 
     for step in range(EARLY[0]):
         pump_p(step)
-    gram_ref[...] = exact_dot(panel_ref[...], panel_ref[...], ((0,), (0,)))
     sends = scatter(gram_ref, rs_ref, rs_send, rs_recv)
     for copy in sends:
         copy.start()
@@ -298,12 +295,13 @@
         both[:, 1].reshape(size, size).T,
         lambda turn: pump_p(done + turn),
     )
-    for step in range(done + turns, total_steps):
+    for step in range(done + turns, steps_p):
         pump_p(step)
     settle(colp, pump_send, pump_recv, in_order, range(CHUNKS))
     linv, upper, coupling = split_factor(work, other)
     band_ref[...] = -upper
     linv_pair = split(linv)
+    coupling_pair = split(coupling)
 
     def unit(start):
         r = lax.broadcasted_iota(jnp.int32, (TILE, size), 0) + start
@@ -413,9 +411,10 @@
         if i < tiles:
             if bits > 1:
                 bit_copy(last, i).wait_recv()
-                prod[side_at(h, i)] = acc[last, small_at(i)] + got[last, small_at(i)]
+                value = acc[last, small_at(i)] + got[last, small_at(i)]
             else:
-                prod[side_at(h, i)] = part[side_at(h, i)] + got[0, small_at(i)]
+                value = part[side_at(h, i)] + got[0, small_at(i)]
+            prod[side_at(h, i)] = pair_dot(split(value), coupling_pair, ((1,), (0,)))
             back_copy(i, h).start()
         if i == tiles // 2:
             for copy in sends:
@@ -442,18 +441,16 @@
         pump_q(step)
         return carry
 
-    lax.fori_loop(CHUNKS, total_steps, rest, 0)
+    lax.fori_loop(CHUNKS, steps_q, rest, 0)
     for copy in arrivals:
         copy.wait_recv()
     inner = exact_dot(both2[...].reshape(size, size), coupling, ((1,), (0,)))
     small = exact_dot(coupling, inner, ((0,), (0,)))
-    coupling_pair = split(coupling)
-    small_pair = split(-0.5 * small)
+    small_pair = split(small)
 
     def row_update(i, carry):
         at = tile_of(i)
-        value = pair_dot(split(prod[at]), coupling_pair, ((1,), (0,)))
-        value = value + pair_dot((left_hi[at, :size], left_lo[at, :size]), small_pair, ((1,), (0,)))
+        value = prod[at] - pair_dot((left_hi[at, :size], left_lo[at, :size]), small_pair, ((1,), (0,)))
         left_hi[at, size:], left_lo[at, size:] = split(value)
         return carry
 
@@ -465,9 +462,7 @@
 
         def col_update(i, carry):
             at = pl.ds(pl.multiple_of(i * half + j * small_rows, small_rows), small_rows)
-            value = pair_dot(split(colq[at]), coupling_pair, ((1,), (0,)))
-            value = value + pair_dot((vcat[at, :size], vcat[at, size:]), small_pair, ((1,), (0,)))
-            right_hi[at, :size], right_lo[at, :size] = split(value)
+            right_hi[at, :size], right_lo[at, :size] = split(colq[at])
             return carry
 
         lax.fori_loop(0, 2 * blocks, col_update, 0)
@@ -505,11 +500,9 @@
             jax.ShapeDtypeStruct((size, size), F32),
             jax.ShapeDtypeStruct((rows, cols), F32),
         ],
-        in_specs=[pl.BlockSpec(memory_space=pltpu.HBM)] * 2,
+        in_specs=[vmem, pl.BlockSpec(memory_space=pltpu.HBM)],
         out_specs=[vmem] * 6,
         scratch_shapes=[
-            pltpu.VMEM((rows, size), F32),
-            dma,
             dma,
             dma,
             pltpu.VMEM((cols, size), F32),

time: 79.1 us -> 70.1 us (0.89)
  the two profiles are of different devices: /device:TPU:0 before, /device:TPU:5 now
where the time goes in v2:
time: 70.1 us; the launch traced here: 69.7 us
  Pallas kernels  68 us (97%)
  local copies, waits for them, and re-layouts  1.03 us (1%)
    pallas_call x1, Pallas kernels, exchange(): pl.pallas_call(functools.partial(exchange_kernel, (n, m, nx, blocks)), ou...  62.3 us
    pallas_call x1, Pallas kernels, finish(): pl.pallas_call(finish_kernel, grid=(cols // tile,), out_shape=[jax.ShapeD...  5.71 us

profile of v2, /device:TPU:5, one launch (start us, length us, event | category | flops | bytes accessed | tf_op | source)
XLA Modules:
  0.0 69.7 jit_solution(4080538994321119327)
XLA Ops:
  0.6 0.0 copy-start
  0.6 1.0 %copy-done = f32[1024,128]{1,0:T(8,128)S(1)} copy-done((f32[1024,128]{1,0:T(8,128)S(1)}, f32[1024,128]{1,0:T(8,128)}, u32[]{:S(2)}) %copy-start) | copy-done | bytes 524312
  1.7 62.3 %exchange.1 = (bf16[1024,256]{1,0:T(8,128)(2,1)S(1)}, bf16[1024,256]{1,0:T(8,128)(2,1)S(1)}, bf16[2048,256]{1,0:T(8,128)(2,1)S(1)}, bf16[2048,256]{1,0:T(8,128)(...) custom-call(f32[1024,128]{1,0:T(8,128)S(1)} %copy-done, f32[1024,2048]{1,0:T(8,128)} %trail_ref.1), custom_call_target="tpu_custom_call" | custom-call | tf_op jit(solution)/shard_map/exchange/pallas_call | solution.py:493
  64.0 5.7 %finish.1 = (f32[1024,2048]{1,0:T(8,128)}, f32[128,128]{1,0:T(8,128)}) custom-call(f32[1024,2048]{1,0:T(8,128)S(1)} %get-tuple-element.8.t_ref, bf16[1024,256]{1,0:T(8,128)(2,1)S(1)} %get-tuple-element.9.lh, bf16[1024,256]{1,0:T(8,128)(2,1)S(1)} %get-tuple-element.10.ll, bf16[2048,256]{1,0:T(8,128)(2,1)S(1)} %get-tuple-element.11.rh, ...), custom_call_target="tpu_custom_call" | custom-call | tf_op jit(solution)/shard_map/finish/pallas_call | solution.py:561
Async XLA Ops:
  0.6 1.0 %copy-start = (f32[1024,128]{1,0:T(8,128)S(1)}, f32[1024,128]{1,0:T(8,128)}, u32[]{:S(2)}) copy-start(f32[1024,128]{1,0:T(8,128)} %panel_ref.1) | copy-start | bytes 1572868

commit v3 on v2

--- a/solution.py
+++ b/solution.py
@@ -58,9 +58,10 @@
 
 MESH = pl.DeviceIdType.MESH
 CHUNKS = 16
-EARLY = (4, 4, 4)
+EARLY = (1, 4, 4)
 SLACK = (4, 4)
 TILE = 256
+PIECE = 64
 PAIR = 4
 GRANT = 24 * 1024 * 1024
 F32 = jnp.float32
@@ -88,7 +89,7 @@
 
 def exchange_kernel(
     sizes, panel_ref, trail_ref, left_hi, left_lo, right_hi, right_lo, band_ref, t_buf,
-    own_sem, t_sem, colp, colq, vcat, part, acc, got, prod, vec,
+    own_sem, t_sem, colp, colq, vcat, t_hi, t_lo, part, acc, got, prod, vec,
     gram_ref, rs_ref, both, small_ref, rs2_ref, pc_ref, both2,
     top_send, top_recv, rs_send, rs_recv, ag_send, ag_recv, rs2_send, rs2_recv, ag2_send, ag2_recv, pc_send, pc_recv,
     pump_send, pump_recv, pump2_send, pump2_recv, red_send, red_recv, bit_send, bit_recv, back_send, back_recv,
@@ -186,27 +187,29 @@
             far = jnp.where(dz < 0, -dz, dz) + jnp.where(dx < 0, -dx, dx)
             c = step - slack * far
 
-            @pl.when(jnp.logical_and(c >= 0, c < CHUNKS))
+            @pl.when(jnp.logical_and(relays(dz, dx), jnp.logical_and(c >= 0, c < CHUNKS)))
             def _():
                 part_of = buf.at[pl.ds(k * rows + where(k, c), chunk_rows)]
 
-                @pl.when(jnp.logical_and(far > 0, relays(dz, dx)))
+                @pl.when(far > 0)
                 def _():
                     remote(part_of, part_of, send.at[k, 0], recv.at[k, c], {"prow": peer(1)}).wait_recv()
 
                 for d, (has, to) in enumerate(children(dz, dx)):
 
-                    @pl.when(jnp.logical_and(has, far > 0))
+                    @pl.when(has if source is None else jnp.logical_and(has, far > 0))
                     def _():
                         remote(part_of, part_of, send.at[k, d], recv.at[k, c], {"prow": to}).start()
 
-                    @pl.when(jnp.logical_and(has, far == 0))
-                    def _():
-                        own = source.at[pl.ds(where(k, c), chunk_rows)]
-                        remote(own, part_of, send.at[k, d], recv.at[k, c], {"prow": to}).start()
+                    if source is not None:
+
+                        @pl.when(jnp.logical_and(has, far == 0))
+                        def _():
+                            own = source.at[pl.ds(where(k, c), chunk_rows)]
+                            remote(own, part_of, send.at[k, d], recv.at[k, c], {"prow": to}).start()
 
     def pump_p(step):
-        pump(step, colp, panel_ref, pump_send, pump_recv, in_order, SLACK[0])
+        pump(step, colp, None, pump_send, pump_recv, in_order, SLACK[0])
 
     def pump_q(step):
         pump(step, colq, prod, pump2_send, pump2_recv, paired, SLACK[1])
@@ -221,7 +224,7 @@
                 def _():
                     remote(whole, whole, send.at[k, d], recv.at[k, 0], {"prow": peer(1)}).wait_send()
 
-    steps_p, steps_q = [CHUNKS + slack * (nz - 1 + max(nx - 1, 0)) for slack in SLACK]
+    steps_p, steps_q = [CHUNKS + slack * (nz - 1 + max(nx - 2, 0)) for slack in SLACK]
 
     def scatter(src, slots, send, recv):
         def copy(offset):
@@ -247,6 +250,14 @@
         for offset in range(1, n):
             value = value + slots[offset]
         return value
+
+    def split_rows(side):
+        def body(i, carry):
+            at = pl.ds(pl.multiple_of(side * half + i * PIECE, PIECE), PIECE)
+            t_hi[at], t_lo[at] = split(t_buf[at])
+            return carry
+
+        lax.fori_loop(0, half // PIECE, body, 0)
 
     def top_copy(j):
         return remote(panel_ref.at[pl.ds(j * piece, piece)], both.at[j, 1], top_send.at[j], top_recv, {"prow": j})
@@ -264,6 +275,8 @@
         copy.start()
     for step in range(EARLY[0], sum(EARLY[:2])):
         pump_p(step)
+    t_copy.wait()
+    split_rows(0)
 
     @pl.when(me > 0)
     def _():
@@ -278,6 +291,7 @@
         copy.start()
     for step in range(sum(EARLY[:2]), sum(EARLY)):
         pump_p(step)
+    split_rows(1)
     for copy in arrivals:
         copy.wait_recv()
     for copy in sends + sends2:
@@ -318,7 +332,6 @@
         return carry
 
     lax.fori_loop(0, blocks * rows // TILE, col_vectors, 0)
-    t_copy.wait()
 
     h = q % 2
     per_half = half // TILE
@@ -333,24 +346,11 @@
     def red_copy(i):
         return remote(part.at[half_at(1 - h, i)], got.at[0, tile_of(i)], red_send.at[i], red_recv.at[i], mate)
 
-    def times(side):
-        def body(i, carry):
-            at = half_at(side, i)
-            high, low = split(t_buf[at])
-            wide = lax.dot_general(high, vcat[...], (((1,), (0,)), ((), ())), preferred_element_type=F32)
-            rest = lax.dot_general(low, vcat[:, :size], (((1,), (0,)), ((), ())), preferred_element_type=F32)
-            part[at] = wide[:, :size] + (wide[:, size:] + rest)
-
-            @pl.when(side != h)
-            def _():
-                red_copy(i).start()
-
-            return carry
-
-        lax.fori_loop(0, per_half, body, 0)
-
-    times(1 - h)
-    times(h)
+    def times(side, i):
+        at = half_at(side, i)
+        wide = lax.dot_general(t_hi[at], vcat[...], (((1,), (0,)), ((), ())), preferred_element_type=F32)
+        rest = lax.dot_general(t_lo[at], vcat[:, :size], (((1,), (0,)), ((), ())), preferred_element_type=F32)
+        part[at] = wide[:, :size] + (wide[:, size:] + rest)
 
     small_rows = PAIR // 2 * chunk_rows
     tiles = half // small_rows
@@ -372,12 +372,20 @@
         at = side_at(side, i)
         return remote(prod.at[at], prod.at[at], back_send.at[i], back_recv.at[i], mate)
 
-    for i in range(per_half):
+    def reduced(i):
         red_copy(i).wait_recv()
         if bits > 1:
             acc[1, tile_of(i)] = part[half_at(h, i)] + got[0, tile_of(i)]
             for j in range(i * TILE // small_rows, (i + 1) * TILE // small_rows):
                 bit_copy(1, j).start()
+
+    for i in range(per_half):
+        times(1 - h, i)
+        red_copy(i).start()
+        if i > 0:
+            reduced(i - 1)
+        times(h, i)
+    reduced(per_half - 1)
 
     def row_vectors(i, carry):
         at = tile_of(i)
@@ -508,6 +516,8 @@
             pltpu.VMEM((cols, size), F32),
             pltpu.VMEM((cols, size), F32),
             pltpu.VMEM((cols, 2 * size), narrow),
+            pltpu.VMEM((rows, cols), narrow),
+            pltpu.VMEM((rows, cols), narrow),
             pltpu.VMEM((rows, size), F32),
             pltpu.VMEM((bits, half, size), F32),
             pltpu.VMEM((bits, half, size), F32),

time: 70.1 us -> 69.1 us (0.986)
    pallas_call x1, Pallas kernels: 62.3 us -> 61.6 us  [exchange(): pl.pallas_call(functools.partial(exchange_kernel, (n, m, nx, blocks)), ou...]
where the time goes in v3:
time: 69.1 us; the launch traced here: 69 us
  Pallas kernels  67.3 us (97%)
  local copies, waits for them, and re-layouts  1.03 us (1%)
    pallas_call x1, Pallas kernels, exchange(): pl.pallas_call(functools.partial(exchange_kernel, (n, m, nx, blocks)), ou...  61.6 us
    pallas_call x1, Pallas kernels, finish(): pl.pallas_call(finish_kernel, grid=(cols // tile,), out_shape=[jax.ShapeD...  5.71 us

profile of v3, /device:TPU:5, one launch (start us, length us, event | category | flops | bytes accessed | tf_op | source)
XLA Modules:
  0.0 69.0 jit_solution(7661695433289730643)
XLA Ops:
  0.6 0.0 copy-start
  0.6 1.0 %copy-done = f32[1024,128]{1,0:T(8,128)S(1)} copy-done((f32[1024,128]{1,0:T(8,128)S(1)}, f32[1024,128]{1,0:T(8,128)}, u32[]{:S(2)}) %copy-start) | copy-done | bytes 524312
  1.7 61.6 %exchange.1 = (bf16[1024,256]{1,0:T(8,128)(2,1)S(1)}, bf16[1024,256]{1,0:T(8,128)(2,1)S(1)}, bf16[2048,256]{1,0:T(8,128)(2,1)S(1)}, bf16[2048,256]{1,0:T(8,128)(...) custom-call(f32[1024,128]{1,0:T(8,128)S(1)} %copy-done, f32[1024,2048]{1,0:T(8,128)} %trail_ref.1), custom_call_target="tpu_custom_call" | custom-call | tf_op jit(solution)/shard_map/exchange/pallas_call | solution.py:501
  63.2 5.7 %finish.1 = (f32[1024,2048]{1,0:T(8,128)}, f32[128,128]{1,0:T(8,128)}) custom-call(f32[1024,2048]{1,0:T(8,128)S(1)} %get-tuple-element.8.t_ref, bf16[1024,256]{1,0:T(8,128)(2,1)S(1)} %get-tuple-element.9.lh, bf16[1024,256]{1,0:T(8,128)(2,1)S(1)} %get-tuple-element.10.ll, bf16[2048,256]{1,0:T(8,128)(2,1)S(1)} %get-tuple-element.11.rh, ...), custom_call_target="tpu_custom_call" | custom-call | tf_op jit(solution)/shard_map/finish/pallas_call | solution.py:571
Async XLA Ops:
  0.6 1.0 %copy-start = (f32[1024,128]{1,0:T(8,128)S(1)}, f32[1024,128]{1,0:T(8,128)}, u32[]{:S(2)}) copy-start(f32[1024,128]{1,0:T(8,128)} %panel_ref.1) | copy-start | bytes 1572868

commit v4 on v3

--- a/solution.py
+++ b/solution.py
@@ -187,11 +187,11 @@
             far = jnp.where(dz < 0, -dz, dz) + jnp.where(dx < 0, -dx, dx)
             c = step - slack * far
 
-            @pl.when(jnp.logical_and(relays(dz, dx), jnp.logical_and(c >= 0, c < CHUNKS)))
+            @pl.when(jnp.logical_and(c >= 0, c < CHUNKS))
             def _():
                 part_of = buf.at[pl.ds(k * rows + where(k, c), chunk_rows)]
 
-                @pl.when(far > 0)
+                @pl.when(jnp.logical_and(far > 0, relays(dz, dx)))
                 def _():
                     remote(part_of, part_of, send.at[k, 0], recv.at[k, c], {"prow": peer(1)}).wait_recv()
 
@@ -224,7 +224,7 @@
                 def _():
                     remote(whole, whole, send.at[k, d], recv.at[k, 0], {"prow": peer(1)}).wait_send()
 
-    steps_p, steps_q = [CHUNKS + slack * (nz - 1 + max(nx - 2, 0)) for slack in SLACK]
+    steps_p, steps_q = [CHUNKS + slack * (nz - 1 + max(nx - 1, 0)) for slack in SLACK]
 
     def scatter(src, slots, send, recv):
         def copy(offset):

time: 69.1 us -> 68.2 us (0.987)
  Pallas kernels: 67.3 us -> 66 us
    pallas_call x1, Pallas kernels: 61.6 us -> 60.2 us  [exchange(): pl.pallas_call(functools.partial(exchange_kernel, (n, m, nx, blocks)), ou...]
where the time goes in v4:
time: 68.2 us; the launch traced here: 67.6 us
  Pallas kernels  66 us (97%)
  local copies, waits for them, and re-layouts  1.03 us (2%)
    pallas_call x1, Pallas kernels, exchange(): pl.pallas_call(functools.partial(exchange_kernel, (n, m, nx, blocks)), ou...  60.2 us
    pallas_call x1, Pallas kernels, finish(): pl.pallas_call(finish_kernel, grid=(cols // tile,), out_shape=[jax.ShapeD...  5.71 us

profile of v4, /device:TPU:5, one launch (start us, length us, event | category | flops | bytes accessed | tf_op | source)
XLA Modules:
  0.0 67.6 jit_solution(2137012139751597815)
XLA Ops:
  0.6 0.0 copy-start
  0.6 1.0 %copy-done = f32[1024,128]{1,0:T(8,128)S(1)} copy-done((f32[1024,128]{1,0:T(8,128)S(1)}, f32[1024,128]{1,0:T(8,128)}, u32[]{:S(2)}) %copy-start) | copy-done | bytes 524312
  1.7 60.2 %exchange.1 = (bf16[1024,256]{1,0:T(8,128)(2,1)S(1)}, bf16[1024,256]{1,0:T(8,128)(2,1)S(1)}, bf16[2048,256]{1,0:T(8,128)(2,1)S(1)}, bf16[2048,256]{1,0:T(8,128)(...) custom-call(f32[1024,128]{1,0:T(8,128)S(1)} %copy-done, f32[1024,2048]{1,0:T(8,128)} %trail_ref.1), custom_call_target="tpu_custom_call" | custom-call | tf_op jit(solution)/shard_map/exchange/pallas_call | solution.py:501
  61.9 5.7 %finish.1 = (f32[1024,2048]{1,0:T(8,128)}, f32[128,128]{1,0:T(8,128)}) custom-call(f32[1024,2048]{1,0:T(8,128)S(1)} %get-tuple-element.8.t_ref, bf16[1024,256]{1,0:T(8,128)(2,1)S(1)} %get-tuple-element.9.lh, bf16[1024,256]{1,0:T(8,128)(2,1)S(1)} %get-tuple-element.10.ll, bf16[2048,256]{1,0:T(8,128)(2,1)S(1)} %get-tuple-element.11.rh, ...), custom_call_target="tpu_custom_call" | custom-call | tf_op jit(solution)/shard_map/finish/pallas_call | solution.py:571
Async XLA Ops:
  0.6 1.0 %copy-start = (f32[1024,128]{1,0:T(8,128)S(1)}, f32[1024,128]{1,0:T(8,128)}, u32[]{:S(2)}) copy-start(f32[1024,128]{1,0:T(8,128)} %panel_ref.1) | copy-start | bytes 1572868
